TPU v7x, 32 devices: a whole 2x2x4 slice. The times are simulated.
32 devices in a mesh: fsdp: 8 (over z, y), seq: 4 (over x, core).
Axes of the slice: x: 2, y: 2, z: 4, core: 2. Of those that a mesh axis runs over, the one named last changes fastest.
Arguments:
- tokens: bfloat16 [16, 1024, 1024], P('fsdp', 'seq'), may hold values from -6 to 6
- first_gain: float32 [1024], replicated, may hold values from 0.5 to 1.5
- first_shift: float32 [1024], replicated, may hold values from -1 to 1
- attention_weight: bfloat16 [1024, 3072], P('fsdp', 'seq'), may hold values from -0.25 to 0.25
- attention_bias: float32 [3072], replicated, may hold values from -1.5 to 1.5
- output_weight: bfloat16 [1024, 1024], P('fsdp', 'seq'), may hold values from -1.5 to 1.5
- output_bias: float32 [1024], replicated, may hold values from -1 to 1
- second_gain: float32 [1024], replicated, may hold values from 0.5 to 1.5
- second_shift: float32 [1024], replicated, may hold values from -1 to 1
- expand_weight: bfloat16 [1024, 4096], P('fsdp', 'seq'), may hold values from -0.1875 to 0.1875
- expand_bias: float32 [4096], replicated, may hold values from -1 to 1
- contract_weight: bfloat16 [4096, 1024], P('fsdp', 'seq'), may hold values from -0.1875 to 0.1875
- contract_bias: float32 [1024], replicated, may hold values from -1 to 1
- cotangent: bfloat16 [16, 1024, 1024], P('fsdp', 'seq'), may hold values from -6 to 6
- threshold: float32 [1], replicated, may hold values from 3 to 6
Outputs:
- block_output: bfloat16 [16, 1024, 1024], P('fsdp', 'seq')
- input_grad: float32 [16, 1024, 1024], P('fsdp', 'seq')
- grad_first_gain: float32 [1024], replicated
- grad_first_shift: float32 [1024], replicated
- grad_attention_weight: float32 [1024, 3072], P('fsdp', 'seq')
- grad_attention_bias: float32 [3072], replicated
- grad_output_weight: float32 [1024, 1024], P('fsdp', 'seq')
- grad_output_bias: float32 [1024], replicated
- grad_second_gain: float32 [1024], replicated
- grad_second_shift: float32 [1024], replicated
- grad_expand_weight: float32 [1024, 4096], P('fsdp', 'seq')
- grad_expand_bias: float32 [4096], replicated
- grad_contract_weight: float32 [4096, 1024], P('fsdp', 'seq')
- grad_contract_bias: float32 [1024], replicated
- head_peak: float32 [16], P('seq')
- clipped_weight: float32 [1024, 3072], P('fsdp', 'seq')
- clipped_bias: float32 [3072], P('seq')
All inputs are finite; a program needn't handle non-finite values.
Results may differ from a plain program's by a relative error of at most 0.018.
Values may be sent and summed in bfloat16 or wider, within the bound.
No kernel may reach another device: no remote copies, remote signals or barrier semaphores. Data moves between devices by JAX's collectives and lax.ppermute only.
A program may use at most 320 MiB of HBM per device.

v0:
```python
import jax
import jax.numpy as jnp
from jax import lax
from jax.sharding import PartitionSpec as P

D = 1024
H = 16
HD = 64
QBLK = 512


def layer_norm(values, gain, shift):
    centered = values - jnp.mean(values, axis=-1, keepdims=True)
    variance = jnp.mean(centered * centered, axis=-1, keepdims=True)
    return centered * lax.rsqrt(variance + 1e-05) * gain + shift


def gelu_tanh(values):
    return jax.nn.gelu(values, approximate=True)


def causal_mask(row_start, row_stop):
    row_ids = row_start + jnp.arange(row_stop - row_start)[:, None]
    col_ids = jnp.arange(row_stop)[None, :]
    return col_ids <= row_ids


def block_logits(query_block, keys_part, row_start, row_stop, logit_scale):
    logits = (
        jnp.einsum("nqhd,nkhd->nhqk", query_block, keys_part, preferred_element_type=jnp.float32)
        * logit_scale
    )
    return jnp.where(causal_mask(row_start, row_stop), logits, -jnp.inf)


def split_packed(packed):
    head_size = packed.shape[-1] // 3
    return (
        packed[..., :head_size],
        packed[..., head_size : 2 * head_size],
        packed[..., 2 * head_size :],
    )


def attend_forward(packed):
    queries, keys_all, values_all = split_packed(packed)
    length = packed.shape[1]
    logit_scale = queries.shape[-1] ** (-0.5)
    outputs = []
    log_sums = []
    peak_value = None
    for block_index in range(length // QBLK):
        row_start = block_index * QBLK
        row_stop = row_start + QBLK
        logits = block_logits(
            queries[:, row_start:row_stop], keys_all[:, :row_stop], row_start, row_stop, logit_scale
        )
        row_top = jnp.max(logits, axis=-1, keepdims=True)
        shifted = jnp.exp(logits - row_top)
        row_total = jnp.sum(shifted, axis=-1, keepdims=True)
        probabilities = (shifted / row_total).astype(jnp.bfloat16)
        block_out = jnp.einsum(
            "nhqk,nkhd->nqhd",
            probabilities,
            values_all[:, :row_stop],
            preferred_element_type=jnp.float32,
        )
        outputs.append(block_out.astype(jnp.bfloat16))
        log_sums.append((row_top + jnp.log(row_total))[..., 0])
        block_peak = jnp.max(row_top[..., 0], axis=-1)
        peak_value = block_peak if peak_value is None else jnp.maximum(peak_value, block_peak)
    return (jnp.concatenate(outputs, axis=1), jnp.concatenate(log_sums, axis=-1), peak_value)


def attend_items(packed):
    attended, log_sums, peak_value = attend_forward(packed)
    returned = lax.all_to_all(attended, "seq", split_axis=1, concat_axis=2, tiled=True)
    return (returned, log_sums, peak_value, packed)


def attend_backward(packed, log_sums, heads_cot):
    queries, keys_all, values_all = split_packed(packed)
    length = packed.shape[1]
    logit_scale = queries.shape[-1] ** (-0.5)
    query_grads = []
    key_grad = jnp.zeros(keys_all.shape, jnp.float32)
    value_grad = jnp.zeros(values_all.shape, jnp.float32)
    for block_index in range(length // QBLK):
        row_start = block_index * QBLK
        row_stop = row_start + QBLK
        query_block = queries[:, row_start:row_stop]
        cot_block = heads_cot[:, row_start:row_stop]
        logits = block_logits(query_block, keys_all[:, :row_stop], row_start, row_stop, logit_scale)
        probabilities = jnp.exp(logits - log_sums[:, :, row_start:row_stop, None])
        prob_grad = jnp.einsum(
            "nqhd,nkhd->nhqk",
            cot_block,
            values_all[:, :row_stop],
            preferred_element_type=jnp.float32,
        )
        row_inner = jnp.sum(prob_grad * probabilities, axis=-1, keepdims=True)
        logit_grad = (probabilities * (prob_grad - row_inner)).astype(jnp.bfloat16)
        query_grads.append(
            jnp.einsum(
                "nhqk,nkhd->nqhd",
                logit_grad,
                keys_all[:, :row_stop],
                preferred_element_type=jnp.float32,
            )
            * logit_scale
        )
        key_grad = key_grad.at[:, :row_stop].add(
            jnp.einsum(
                "nhqk,nqhd->nkhd", logit_grad, query_block, preferred_element_type=jnp.float32
            )
            * logit_scale
        )
        value_grad = value_grad.at[:, :row_stop].add(
            jnp.einsum(
                "nhqk,nqhd->nkhd",
                probabilities.astype(jnp.bfloat16),
                cot_block,
                preferred_element_type=jnp.float32,
            )
        )
    joined = jnp.concatenate([jnp.concatenate(query_grads, axis=1), key_grad, value_grad], axis=-1)
    return joined.astype(jnp.bfloat16)


def body(
    tokens,
    first_gain,
    first_shift,
    attention_weight,
    attention_bias,
    output_weight,
    output_bias,
    second_gain,
    second_shift,
    expand_weight,
    expand_bias,
    contract_weight,
    contract_bias,
    cotangent,
    threshold,
):
    partial_full = (
        lax.all_gather(attention_weight, "seq", axis=1, tiled=True),
        lax.all_gather(output_weight, "seq", axis=1, tiled=True),
        lax.all_gather(expand_weight, "seq", axis=1, tiled=True),
        lax.all_gather(contract_weight, "seq", axis=1, tiled=True),
    )
    full_weights = (
        lax.all_gather(partial_full[0], "fsdp", axis=0, tiled=True),
        lax.all_gather(partial_full[1], "fsdp", axis=0, tiled=True),
        lax.all_gather(partial_full[2], "fsdp", axis=0, tiled=True),
        lax.all_gather(partial_full[3], "fsdp", axis=0, tiled=True),
    )
    mixing_full, output_full, expand_full, contract_full = full_weights
    seq_here = tokens.shape[0]
    tok_here = tokens.shape[1]
    tokens_float = tokens.astype(jnp.float32)
    normed_first = layer_norm(tokens_float, first_gain, first_shift).astype(jnp.bfloat16)
    mixed = (
        jnp.einsum("ntd,de->nte", normed_first, mixing_full, preferred_element_type=jnp.float32)
        + attention_bias
    )
    mixed = mixed.astype(jnp.bfloat16).reshape(seq_here, tok_here, H, 3 * HD)
    returned, log_sums, peaks, packed = attend_items(
        lax.all_to_all(mixed, "seq", split_axis=2, concat_axis=1, tiled=True)
    )
    attended = returned.reshape(seq_here, tok_here, D)
    residual = (
        tokens_float
        + jnp.einsum("nte,ed->ntd", attended, output_full, preferred_element_type=jnp.float32)
        + output_bias
    )
    normed_second = layer_norm(residual, second_gain, second_shift).astype(jnp.bfloat16)
    hidden = (
        jnp.einsum("ntd,di->nti", normed_second, expand_full, preferred_element_type=jnp.float32)
        + expand_bias
    )
    active = gelu_tanh(hidden).astype(jnp.bfloat16)
    result = (
        residual
        + jnp.einsum("nti,id->ntd", active, contract_full, preferred_element_type=jnp.float32)
        + contract_bias
    )
    block_output = result.astype(jnp.bfloat16)
    cot_float = cotangent.astype(jnp.float32)
    grad_contract = jnp.einsum("nti,ntd->id", active, cotangent, preferred_element_type=jnp.float32)
    grad_contract_bias = jnp.sum(cot_float, axis=(0, 1))
    active_cot = jnp.einsum(
        "ntd,id->nti", cotangent, contract_full, preferred_element_type=jnp.float32
    )
    _, gelu_pull = jax.vjp(gelu_tanh, hidden)
    hidden_cot = gelu_pull(active_cot)[0].astype(jnp.bfloat16)
    grad_expand = jnp.einsum(
        "ntd,nti->di", normed_second, hidden_cot, preferred_element_type=jnp.float32
    )
    grad_expand_bias = jnp.sum(hidden_cot.astype(jnp.float32), axis=(0, 1))
    second_cot = jnp.einsum(
        "nti,di->ntd", hidden_cot, expand_full, preferred_element_type=jnp.float32
    )
    _, second_pull = jax.vjp(layer_norm, residual, second_gain, second_shift)
    residual_part, grad_second_gain, grad_second_shift = second_pull(second_cot)
    residual_cot = cot_float + residual_part
    branch_cot = residual_cot.astype(jnp.bfloat16)
    grad_output = jnp.einsum(
        "nte,ntd->ed", attended, branch_cot, preferred_element_type=jnp.float32
    )
    grad_output_bias = jnp.sum(branch_cot.astype(jnp.float32), axis=(0, 1))
    attended_cot = jnp.einsum(
        "ntd,ed->nte", branch_cot, output_full, preferred_element_type=jnp.float32
    )
    attended_cot = attended_cot.astype(jnp.bfloat16).reshape(seq_here, tok_here, H, HD)
    heads_cot = lax.all_to_all(attended_cot, "seq", split_axis=2, concat_axis=1, tiled=True)
    packed_cot = attend_backward(packed, log_sums, heads_cot)
    mixed_cot = lax.all_to_all(packed_cot, "seq", split_axis=1, concat_axis=2, tiled=True).reshape(
        seq_here, tok_here, 3 * D
    )
    grad_mixing = jnp.einsum(
        "ntd,nte->de", normed_first, mixed_cot, preferred_element_type=jnp.float32
    )
    grad_mixing_bias = jnp.sum(mixed_cot.astype(jnp.float32), axis=(0, 1))
    first_cot = jnp.einsum(
        "nte,de->ntd", mixed_cot, mixing_full, preferred_element_type=jnp.float32
    )
    _, first_pull = jax.vjp(layer_norm, tokens_float, first_gain, first_shift)
    token_part, grad_first_gain, grad_first_shift = first_pull(first_cot)
    input_grad = residual_cot + token_part
    summed_first = (
        lax.psum_scatter(
            grad_mixing.astype(jnp.bfloat16), "fsdp", scatter_dimension=0, tiled=True
        ).astype(jnp.float32),
        lax.psum_scatter(
            grad_output.astype(jnp.bfloat16), "fsdp", scatter_dimension=0, tiled=True
        ).astype(jnp.float32),
        lax.psum_scatter(
            grad_expand.astype(jnp.bfloat16), "fsdp", scatter_dimension=0, tiled=True
        ).astype(jnp.float32),
        lax.psum_scatter(
            grad_contract.astype(jnp.bfloat16), "fsdp", scatter_dimension=0, tiled=True
        ).astype(jnp.float32),
    )
    weight_grads = (
        lax.psum_scatter(
            summed_first[0].astype(jnp.bfloat16), "seq", scatter_dimension=1, tiled=True
        ).astype(jnp.float32),
        lax.psum_scatter(
            summed_first[1].astype(jnp.bfloat16), "seq", scatter_dimension=1, tiled=True
        ).astype(jnp.float32),
        lax.psum_scatter(
            summed_first[2].astype(jnp.bfloat16), "seq", scatter_dimension=1, tiled=True
        ).astype(jnp.float32),
        lax.psum_scatter(
            summed_first[3].astype(jnp.bfloat16), "seq", scatter_dimension=1, tiled=True
        ).astype(jnp.float32),
    )
    vector_totals = lax.psum(
        (
            grad_first_gain,
            grad_first_shift,
            grad_mixing_bias,
            grad_output_bias,
            grad_second_gain,
            grad_second_shift,
            grad_expand_bias,
            grad_contract_bias,
        ),
        ("fsdp", "seq"),
    )
    head_peak = lax.pmax(jnp.max(peaks, axis=0), "fsdp")
    rows_here = attention_weight.shape[0]
    col_width = attention_weight.shape[1]
    heads_here = head_peak.shape[0]
    head_size = col_width // (3 * heads_here)
    factor = jnp.sqrt(threshold[0] / jnp.maximum(head_peak, threshold[0]))
    multiplier = jnp.stack([factor, factor, jnp.ones_like(factor)], axis=1)
    clipped_weight = (
        attention_weight.astype(jnp.float32).reshape(rows_here, heads_here, 3, head_size)
        * multiplier[None, :, :, None]
    ).reshape(rows_here, col_width)
    bias_piece = lax.dynamic_slice_in_dim(
        attention_bias, lax.axis_index("seq") * col_width, col_width
    )
    clipped_bias = (bias_piece.reshape(heads_here, 3, head_size) * multiplier[:, :, None]).reshape(
        col_width
    )
    return (
        block_output,
        input_grad,
        vector_totals[0],
        vector_totals[1],
        weight_grads[0],
        vector_totals[2],
        weight_grads[1],
        vector_totals[3],
        vector_totals[4],
        vector_totals[5],
        weight_grads[2],
        vector_totals[6],
        weight_grads[3],
        vector_totals[7],
        head_peak,
        clipped_weight,
        clipped_bias,
    )


def solution(mesh):
    placed = (
        P("fsdp", "seq", None),
        P(),
        P(),
        P("fsdp", "seq"),
        P(),
        P("fsdp", "seq"),
        P(),
        P(),
        P(),
        P("fsdp", "seq"),
        P(),
        P("fsdp", "seq"),
        P(),
        P("fsdp", "seq", None),
        P(),
    )
    return jax.shard_map(
        body,
        mesh=mesh,
        in_specs=placed,
        out_specs=(
            P("fsdp", "seq", None),
            P("fsdp", "seq", None),
            P(),
            P(),
            P("fsdp", "seq"),
            P(),
            P("fsdp", "seq"),
            P(),
            P(),
            P(),
            P("fsdp", "seq"),
            P(),
            P("fsdp", "seq"),
            P(),
            P("seq"),
            P("fsdp", "seq"),
            P("seq"),
        ),
        check_vma=False,
    )
```

profile of v0, /device:TPU:0, one launch (start us, length us, event | category | flops | bytes accessed | tf_op | source)
XLA Modules:
  0.0 1167.2 jit_solution(12801582693143362905)
XLA Ops:
  8.8 11.7 %all_gather.24 = bf16[128,3072]{1,0:T(8,128)(2,1)} all-gather(bf16[128,768]{1,0:T(8,128)(2,1)} %param.30), channel_id=1, replica_groups=mesh['fsdp'=8,'seq'=4] {'seq'}, dimensions={1}, use_global_device_ids=true | all-gather | bytes 983040 | tf_op jit(solution)/shard_map/all_gather | solution.py:148
  20.5 8.3 all_gather.26
  30.6 18.4 %all-gather.15.cloned.1.call-done = bf16[512,1024]{1,0:T(8,128)(2,1)} async-done(((bf16[512,256]{1,0:T(8,128)(2,1)}), bf16[512,1024]{1,0:T(8,128)(2,1)}) %all-gather.15.cloned.1.call-update) | async-done | bytes 1048592 | tf_op jit(solution)/shard_map/all_gather | solution.py:151
  49.6 100.5 %all-gather.7.cloned.1.call-done = bf16[1024,3072]{1,0:T(8,128)(2,1)} async-done(((bf16[128,3072]{1,0:T(8,128)(2,1)}), bf16[1024,3072]{1,0:T(8,128)(2,1)}) %all-gather.7.cloned.1.call-update) | async-done | bytes 6291472 | tf_op jit(solution)/shard_map/all_gather | solution.py:154
  150.2 7.8 add_convert_fusion
  158.0 4.7 copy.155
  162.8 4.0 copy.156
  166.7 5.0 all-to-all-start
  172.2 36.5 %all-to-all-done = bf16[2,256,16,192]{1,3,0,2:T(8,128)(2,1)} async-done(((bf16[2,256,16,192]{1,3,0,2:T(8,128)(2,1)}), bf16[2,256,16,192]{1,3,0,2:T(8,128)(2,1)}, u32[]{:S(2)}, u32[]{:S(2)}) %all-to-all-start) | async-done | bytes 3145760 | tf_op jit(solution)/shard_map/all_to_all | solution.py:170
  208.7 6.3 copy.158
  215.0 6.1 all_to_all.51
  231.1 3.7 fusion
  236.8 4.5 fusion.73
  248.0 18.9 %all_to_all.66 = bf16[4,2,65536]{2,1,0:T(2,128)(2,1)} all-to-all(bf16[4,2,65536]{2,1,0:T(2,128)(2,1)} %reshape.309), channel_id=1, replica_groups=mesh['fsdp'=8,'seq'=4] {'seq'}, dimensions={0} | all-to-all | bytes 2097152 | tf_op jit(solution)/shard_map/all_to_all | solution.py:77
  276.3 48.9 %all-gather.13.cloned.1.call-done = bf16[1024,4096]{1,0:T(8,128)(2,1)} async-done(((bf16[128,4096]{1,0:T(8,128)(2,1)}), bf16[1024,4096]{1,0:T(8,128)(2,1)}) %all-gather.13.cloned.1.call-update) | async-done | bytes 8388624 | tf_op jit(solution)/shard_map/all_gather | solution.py:156
  325.2 10.2 fusion.17
  335.4 114.9 %all-gather.17.cloned.1.call-done = bf16[4096,1024]{1,0:T(8,128)(2,1)} async-done(((bf16[512,1024]{1,0:T(8,128)(2,1)}), bf16[4096,1024]{1,0:T(8,128)(2,1)}) %all-gather.17.cloned.1.call-update) | async-done | bytes 8388624 | tf_op jit(solution)/shard_map/all_gather | solution.py:157
  450.4 14.6 %convert_reduce_fusion = (f32[4096]{0:T(1024)}, bf16[2,256,4096]{2,1,0:T(8,128)(2,1)S(1)}) fusion(f32[2,256,4096]{2,1,0:T(8,128)} %fusion.17, f32[4096]{0:T(1024)S(1)} %copy-done.41, bf16[2,256,1024]{2,1,0:T(8,128)(2,1)} %param.40, bf16[4096,1024]{1,0:T(8,128)(2,1)} %all-gather.17.cloned.1.call-done), kind=kOutput, calls=%fused_computation.29 | convolution fusion | flops 4343197696 | bytes 22052864 | tf_op jit(solution)/shard_map/ntd,id->nti/dot_general | solution.py:193
  465.0 5.5 multiply_reduce_fusion.2
  478.8 3.5 all-to-all-start.2
  483.0 3.8 bitcast_convert_fusion.3
  486.9 9.9 all-to-all-done.2
  500.5 6.3 fusion.62
  506.7 7.6 fusion.99
  514.4 4.9 multiply_convert_fusion.1
  519.3 3.5 fusion.71
  522.8 3.4 fusion.65
  526.2 10.9 fusion.98
  537.1 7.9 multiply_convert_fusion
  545.0 4.7 fusion.72
  549.7 4.0 fusion.48
  553.8 4.4 fusion.47
  560.0 7.6 copy.170
  567.6 53.8 %all_to_all.67 = bf16[2,1024,4,192]{3,2,0,1:T(4,128)(2,1)} all-to-all(bf16[2,1024,4,192]{3,2,0,1:T(4,128)(2,1)} %copy.170), channel_id=1, replica_groups=mesh['fsdp'=8,'seq'=4] {'seq'}, dimensions={1} | all-to-all | bytes 6291456 | tf_op jit(solution)/shard_map/all_to_all | solution.py:219
  621.5 7.3 copy.172
  628.7 7.7 bitcast_convert_fusion.2
  637.7 13.1 %bitcast_convert_fusion = bf16[4096,1024]{1,0:T(8,128)(2,1)} fusion(bf16[2,256,1024]{2,1,0:T(8,128)(2,1)S(1)} %copy-done.12, f32[2,256,4096]{2,1,0:T(8,128)} %fusion.17, f32[4096]{0:T(1024)S(1)} %copy-done.42), kind=kOutput, calls=%fused_computation | convolution fusion | flops 4320133120 | bytes 17842176 | tf_op jit(solution)/shard_map/nti,ntd->id/dot_general | solution.py:191
  652.4 9.5 bitcast_convert_fusion.1
  662.7 89.2 %reduce-scatter.9.cloned.1.call-done = bf16[128,3072]{1,0:T(8,128)(2,1)} async-done(((bf16[1024,3072]{1,0:T(8,128)(2,1)}), bf16[128,3072]{1,0:T(8,128)(2,1)}) %reduce-scatter.9.cloned.1.call-update) | async-done | bytes 786448 | tf_op jit(solution)/shard_map/reduce_scatter | solution.py:233
  752.7 151.0 %reduce-scatter.21.cloned.1.call-done = bf16[512,1024]{1,0:T(8,128)(2,1)} async-done(((bf16[4096,1024]{1,0:T(8,128)(2,1)}), bf16[512,1024]{1,0:T(8,128)(2,1)}) %reduce-scatter.21.cloned.1.call-update) | async-done | bytes 1048592 | tf_op jit(solution)/shard_map/reduce_scatter | solution.py:242
  903.8 12.2 %add_convert_fusion.1 = bf16[2,256,1024]{2,1,0:T(8,128)(2,1)} fusion(f32[2,256,1024]{2,1,0:T(8,128)S(1)} %copy-done.6, bf16[4096,1024]{1,0:T(8,128)(2,1)} %all-gather.17.cloned.1.call-done, f32[1024]{0:T(1024)S(1)} %copy-done.47, f32[2,256,4096]{2,1,0:T(8,128)} %fusion.17, f32[4096]{0:T(1024)S(1)} %copy-done.42), kind=kOutput, calls=%fused_computation.83 | convolution fusion | flops 4317511680 | bytes 19943424 | tf_op jit(solution)/shard_map/nti,id->ntd/dot_general | solution.py:186
  916.0 20.6 %pmax.7 = f32[4]{0:T(128)S(1)} all-reduce(f32[4]{0:T(128)S(1)} %maximum_reduce_fusion), channel_id=1, replica_groups=mesh['fsdp'=8,'seq'=4] {'fsdp'}, use_global_device_ids=true, to_apply=%region_41.42 | all-reduce | flops 4 | bytes 32 | tf_op jit(solution)/shard_map/pmax | solution.py:273
  939.2 8.0 copy.193
  950.7 105.3 %reduce-scatter.17.cloned.1.call-done = bf16[128,4096]{1,0:T(8,128)(2,1)} async-done(((bf16[1024,4096]{1,0:T(8,128)(2,1)}), bf16[128,4096]{1,0:T(8,128)(2,1)}) %reduce-scatter.17.cloned.1.call-update) | async-done | bytes 1048592 | tf_op jit(solution)/shard_map/reduce_scatter | solution.py:239
  1056.0 7.0 fusion.100
  1066.7 40.8 %all-reduce.2 = (f32[1024]{0:T(1024)}, f32[1024]{0:T(1024)}, f32[3072]{0:T(1024)}, f32[1024]{0:T(1024)}, f32[1024]{0:T(1024)}, /*index=5*/f32[1024]{0:T(1024)}, f32[4096]{0:T(1024)}, f32[1024]{0:T(1024)}) all-reduce(f32[1024]{0:T(1024)S(1)} %get-tuple-element.87, ...), channel_id=1, replica_groups=mesh['fsdp'=8,'seq'=4] {'fsdp','seq'}, use_global_device_ids=true, to_apply=%region_15.16 | all-reduce | flops 13312 | bytes 106496 | tf_op jit(solution)/shard_map/psum | solution.py:260
  1110.7 20.5 %reduce-scatter.23.cloned.1.call-done = bf16[512,256]{1,0:T(8,128)(2,1)} async-done(((bf16[512,1024]{1,0:T(8,128)(2,1)}), bf16[512,256]{1,0:T(8,128)(2,1)}) %reduce-scatter.23.cloned.1.call-update) | async-done | bytes 262160 | tf_op jit(solution)/shard_map/reduce_scatter | solution.py:256
  1133.0 25.7 %reduce-scatter.19.cloned.1.call-done = bf16[128,1024]{1,0:T(8,128)(2,1)} async-done(((bf16[128,4096]{1,0:T(8,128)(2,1)}), bf16[128,1024]{1,0:T(8,128)(2,1)}) %reduce-scatter.19.cloned.1.call-update) | async-done | bytes 262160 | tf_op jit(solution)/shard_map/reduce_scatter | solution.py:253
  (199 shorter events, 67.3 us)
Async XLA Ops:
  7.2 41.8 %copy-start.2 = (bf16[2,256,1024]{2,1,0:T(8,128)(2,1)S(1)}, bf16[2,256,1024]{2,1,0:T(8,128)(2,1)}, u32[]{:S(2)}) copy-start(bf16[2,256,1024]{2,1,0:T(8,128)(2,1)} %param.27) | copy-start | bytes 3145732
  7.2 143.0 %copy-start.28 = (f32[1024]{0:T(1024)S(1)}, f32[1024]{0:T(1024)}, u32[]{:S(2)}) copy-start(f32[1024]{0:T(1024)} %param.28) | copy-start | bytes 12292
  7.2 143.0 %copy-start.39 = (f32[3072]{0:T(1024)S(1)}, f32[3072]{0:T(1024)}, u32[]{:S(2)}) copy-start(f32[3072]{0:T(1024)} %param.31) | copy-start | bytes 36868
  7.2 143.0 %copy-start.43 = (f32[1024]{0:T(1024)S(1)}, f32[1024]{0:T(1024)}, u32[]{:S(2)}) copy-start(f32[1024]{0:T(1024)} %param.29) | copy-start | bytes 12292
  7.2 23.3 %all-gather.11.cloned.1.call-start = ((), (), s32[]{:S(2)}) async-start(), calls=%async_computation.14 | async-start | bytes 1310720 | tf_op jit(solution)/shard_map/all_gather | solution.py:150
  8.0 41.0 %all-gather.15.cloned.1.call-start = ((), (), s32[]{:S(2)}) async-start(), calls=%async_computation.16 | async-start | bytes 1310720 | tf_op jit(solution)/shard_map/all_gather | solution.py:151
  8.7 141.5 %all-gather.7.cloned.1.call-start = ((), (), s32[]{:S(2)}) async-start(), calls=%async_computation.12 | async-start | bytes 7077888 | tf_op jit(solution)/shard_map/all_gather | solution.py:154
  20.5 252.2 %all-gather.9.cloned.1.call-start = ((), (), s32[]{:S(2)}) async-start(), calls=%async_computation.13 | async-start | bytes 2359296 | tf_op jit(solution)/shard_map/all_gather | solution.py:155
  28.9 296.4 %all-gather.13.cloned.1.call-start = ((), (), s32[]{:S(2)}) async-start(), calls=%async_computation.15 | async-start | bytes 9437184 | tf_op jit(solution)/shard_map/all_gather | solution.py:156
  30.5 419.8 %all-gather.17.cloned.1.call-start = ((), (), s32[]{:S(2)}) async-start(), calls=%async_computation.17 | async-start | bytes 9437184 | tf_op jit(solution)/shard_map/all_gather | solution.py:157
  49.2 108.8 %copy-start.21 = (f32[2,256]{1,0:T(2,128)}, f32[2,256]{1,0:T(2,128)S(1)}, u32[]{:S(2)}) copy-start(f32[2,256]{1,0:T(2,128)S(1)} %broadcast_multiply_fusion.1) | copy-start | bytes 6148
  49.6 108.4 %copy-start.25 = (f32[2,256]{1,0:T(2,128)}, f32[2,256]{1,0:T(2,128)S(1)}, u32[]{:S(2)}) copy-start(f32[2,256]{1,0:T(2,128)S(1)} %fusion.44) | copy-start | bytes 6148
  49.6 108.4 %copy-start.23 = (f32[2,256]{1,0:T(2,128)}, f32[2,256]{1,0:T(2,128)S(1)}, u32[]{:S(2)}) copy-start(f32[2,256]{1,0:T(2,128)S(1)} %fusion.96) | copy-start | bytes 6148
  166.7 42.0 %all-to-all-start = ((bf16[2,256,16,192]{1,3,0,2:T(8,128)(2,1)}), bf16[2,256,16,192]{1,3,0,2:T(8,128)(2,1)}, u32[]{:S(2)}, u32[]{:S(2)}) async-start(bf16[2,256,16,192]{1,3,0,2:T(8,128)(2,1)} %copy.156), calls=%async_computation | async-start | bytes 6291456 | tf_op jit(solution)/shard_map/all_to_all | solution.py:170
  223.8 11.0 copy-start.1
  248.0 24.6 %copy-start.27 = (f32[1024]{0:T(1024)S(1)}, f32[1024]{0:T(1024)}, u32[]{:S(2)}) copy-start(f32[1024]{0:T(1024)} %param.33) | copy-start | bytes 12292
  272.6 52.6 %copy-start.37 = (f32[1024]{0:T(1024)S(1)}, f32[1024]{0:T(1024)}, u32[]{:S(2)}) copy-start(f32[1024]{0:T(1024)} %param.34) | copy-start | bytes 12292
  272.6 52.6 %copy-start.45 = (f32[1024]{0:T(1024)S(1)}, f32[1024]{0:T(1024)}, u32[]{:S(2)}) copy-start(f32[1024]{0:T(1024)} %param.35) | copy-start | bytes 12292
  275.9 194.5 %copy-start.5 = (f32[2,256,1024]{2,1,0:T(8,128)}, f32[2,256,1024]{2,1,0:T(8,128)S(1)}, u32[]{:S(2)}) copy-start(f32[2,256,1024]{2,1,0:T(8,128)S(1)} %get-tuple-element.111) | copy-start | bytes 6291460
  276.3 194.1 %copy-start.31 = (f32[2,256]{1,0:T(2,128)}, f32[2,256]{1,0:T(2,128)S(1)}, u32[]{:S(2)}) copy-start(f32[2,256]{1,0:T(2,128)S(1)} %fusion.97) | copy-start | bytes 6148
  276.3 174.0 %copy-start.41 = (f32[4096]{0:T(1024)S(1)}, f32[4096]{0:T(1024)}, u32[]{:S(2)}) copy-start(f32[4096]{0:T(1024)} %param.37) | copy-start | bytes 49156
  450.4 14.6 %copy-start.40 = (bf16[1024,4096]{1,0:T(8,128)(2,1)S(1)}, bf16[1024,4096]{1,0:T(8,128)(2,1)}, u32[]{:S(2)}) copy-start(bf16[1024,4096]{1,0:T(8,128)(2,1)} %all-gather.13.cloned.1.call-done) | copy-start | bytes 25165828
  478.8 18.0 %all-to-all-start.2 = ((bf16[2,256,16,64]{1,3,0,2:T(8,128)(2,1)}), bf16[2,256,16,64]{1,3,0,2:T(8,128)(2,1)S(1)}, u32[]{:S(2)}, u32[]{:S(2)}) async-start(bf16[2,256,16,64]{1,3,0,2:T(8,128)(2,1)} %copy.165), calls=%async_computation.2 | async-start | bytes 2097152 | tf_op jit(solution)/shard_map/all_to_all | solution.py:217
  482.3 179.7 %reduce-scatter.13.cloned.1.call-start = ((), (), s32[]{:S(2)}) async-start(), calls=%async_computation.20 | async-start | bytes 2359296 | tf_op jit(solution)/shard_map/reduce_scatter | solution.py:236
  486.8 265.1 %reduce-scatter.9.cloned.1.call-start = ((), (), s32[]{:S(2)}) async-start(), calls=%async_computation.18 | async-start | bytes 7077888 | tf_op jit(solution)/shard_map/reduce_scatter | solution.py:233
  500.5 13.9 %slice-start.4 = ((s8[8388608]{0:T(1024)(128)(4,1)}), s8[4194304]{0:T(1024)(128)(4,1)S(1)}, s32[]{:S(2)}) async-start(s8[8388608]{0:T(1024)(128)(4,1)} %bitcast.119), calls=%async_computation.30 | async-start | bytes 8388608
  506.7 7.6 slice-start.5
  514.4 11.8 %slice-start = ((s8[16777216]{0:T(1024)(128)(4,1)}), s8[4194304]{0:T(1024)(128)(4,1)S(1)}, s32[]{:S(2)}) async-start(s8[16777216]{0:T(1024)(128)(4,1)} %bitcast.117), calls=%async_computation.26 | async-start | bytes 8388608
  514.4 11.8 %slice-start.1 = ((s8[16777216]{0:T(1024)(128)(4,1)}), s8[4194304]{0:T(1024)(128)(4,1)S(1)}, s32[]{:S(2)}) async-start(s8[16777216]{0:T(1024)(128)(4,1)} %bitcast.117), calls=%async_computation.27 | async-start | bytes 8388608
  514.4 11.8 %slice-start.2 = ((s8[16777216]{0:T(1024)(128)(4,1)}), s8[4194304]{0:T(1024)(128)(4,1)S(1)}, s32[]{:S(2)}) async-start(s8[16777216]{0:T(1024)(128)(4,1)} %bitcast.117), calls=%async_computation.28 | async-start | bytes 8388608
  519.3 6.9 slice-start.3
  621.4 7.3 copy-start.22
  621.4 7.3 copy-start.24
  621.5 7.3 copy-start.29
  621.5 7.3 copy-start.44
  636.5 267.2 %reduce-scatter.21.cloned.1.call-start = ((), (), s32[]{:S(2)}) async-start(), calls=%async_computation.24 | async-start | bytes 9437184 | tf_op jit(solution)/shard_map/reduce_scatter | solution.py:242
  650.8 405.1 %reduce-scatter.17.cloned.1.call-start = ((), (), s32[]{:S(2)}) async-start(), calls=%async_computation.22 | async-start | bytes 9437184 | tf_op jit(solution)/shard_map/reduce_scatter | solution.py:239
  661.9 90.8 %copy-start.33 = (f32[2,4]{1,0:T(2,128)S(1)}, f32[2,4]{1,0:T(2,128)}, u32[]{:S(2)}) copy-start(f32[2,4]{1,0:T(2,128)} %get-tuple-element.83) | copy-start | bytes 100
  661.9 90.8 %copy-start.34 = (f32[2,4]{1,0:T(2,128)S(1)}, f32[2,4]{1,0:T(2,128)}, u32[]{:S(2)}) copy-start(f32[2,4]{1,0:T(2,128)} %get-tuple-element.81) | copy-start | bytes 100
  661.9 241.9 %copy-start.47 = (f32[1024]{0:T(1024)S(1)}, f32[1024]{0:T(1024)}, u32[]{:S(2)}) copy-start(f32[1024]{0:T(1024)} %param.39) | copy-start | bytes 12292
  661.9 445.6 %reduce-scatter.15.cloned.1.call-start = ((), (), s32[]{:S(2)}) async-start(), calls=%async_computation.21 | async-start | bytes 327680 | tf_op jit(solution)/shard_map/reduce_scatter | solution.py:250
  662.6 446.4 %reduce-scatter.11.cloned.1.call-start = ((), (), s32[]{:S(2)}) async-start(), calls=%async_computation.19 | async-start | bytes 983040 | tf_op jit(solution)/shard_map/reduce_scatter | solution.py:247
  751.9 379.3 %reduce-scatter.23.cloned.1.call-start = ((), (), s32[]{:S(2)}) async-start(), calls=%async_computation.25 | async-start | bytes 1310720 | tf_op jit(solution)/shard_map/reduce_scatter | solution.py:256
  903.7 34.6 %copy-start.19 = (bf16[128,768]{1,0:T(8,128)(2,1)S(1)}, bf16[128,768]{1,0:T(8,128)(2,1)}, u32[]{:S(2)}) copy-start(bf16[128,768]{1,0:T(8,128)(2,1)} %param.30) | copy-start | bytes 589828
  903.8 255.0 %reduce-scatter.19.cloned.1.call-start = ((), (), s32[]{:S(2)}) async-start(), calls=%async_computation.23 | async-start | bytes 1310720 | tf_op jit(solution)/shard_map/reduce_scatter | solution.py:253
  936.7 13.7 %copy-start.48 = (f32[4]{0:T(128)}, f32[4]{0:T(128)S(1)}, u32[]{:S(2)}) copy-start(f32[4]{0:T(128)S(1)} %pmax.7) | copy-start | bytes 52
  1056.0 7.0 copy-start.26
  1056.0 8.1 copy-start.13
  (24 other events, 74.5 us)
Sparse Core Ops, SparseCore 0:
  9.6 20.8 all-gather.10
  32.0 16.8 all-gather.14
  51.1 99.0 all-gather.6
  152.2 47.6 all-gather.8
  201.8 123.4 all-gather.12
  327.2 123.0 all-gather.16
  486.9 66.2 reduce-scatter.12
  636.6 115.1 reduce-scatter.8
  755.5 148.1 reduce-scatter.20
  907.6 148.2 reduce-scatter.16
  1058.4 19.0 reduce-scatter.14
  1080.1 23.4 reduce-scatter.10
  1106.1 25.0 reduce-scatter.22
  1133.8 24.9 reduce-scatter.18
where the time goes:
time: 1170 us
  waiting for transfers between devices  725 us (62%)
  blocking collectives  154 us (13%)
  matrix products  153 us (13%)
  local copies, waits for them, and re-layouts  71.4 us (6%)
  other arithmetic  39.2 us (3%)
  between operations  15.3 us (1%)
    reduce_scatter x1, waiting for transfers between devices, body(): lax.psum_scatter(grad_contract.astype(jnp.bfloat16), 'fsdp', scatter_dime...  151 us
    all_gather x1, waiting for transfers between devices, body(): lax.all_gather(partial_full[3], 'fsdp', axis=0, tiled=True)  115 us
    reduce_scatter x1, waiting for transfers between devices, body(): lax.psum_scatter(grad_expand.astype(jnp.bfloat16), 'fsdp', scatter_dimens...  105 us
    all_gather x1, waiting for transfers between devices, body(): lax.all_gather(partial_full[0], 'fsdp', axis=0, tiled=True)  101 us
    reduce_scatter x1, waiting for transfers between devices, body(): lax.psum_scatter(grad_mixing.astype(jnp.bfloat16), 'fsdp', scatter_dimens...  89.2 us
    all_to_all x1, blocking collectives, body(): lax.all_to_all(packed_cot, 'seq', split_axis=1, concat_axis=2, tiled=True)  53.8 us
    all_gather x1, waiting for transfers between devices, body(): lax.all_gather(partial_full[2], 'fsdp', axis=0, tiled=True)  48.9 us
    psum x1, blocking collectives, body(): lax.psum((grad_first_gain, grad_first_shift, grad_mixing_bias, grad_outpu...  40.8 us
  transfers between devices with their start and end apart: 16, of which 12 were waited for; matrix products, arithmetic and copies ran while one was open for 19% of the time, Pallas kernels for 0%

commit v1 on v0

--- a/solution.py
+++ b/solution.py
@@ -7,6 +7,28 @@
 H = 16
 HD = 64
 QBLK = 512
+
+
+def joined_along(tiles, dim):
+    tiles = jnp.moveaxis(tiles, 0, dim)
+    lengths = tiles.shape
+    return tiles.reshape(*lengths[:dim], lengths[dim] * lengths[dim + 1], *lengths[dim + 2 :])
+
+
+def collect(x, axis, dim):
+    devices = lax.axis_size(axis)
+    pairs = [(i, (i + 1) % devices) for i in range(devices)]
+    back = [(b, a) for a, b in pairs]
+    lower, upper = ([], [])
+    for step in range(devices - 1):
+        if step % 2 == 0:
+            lower.append(lax.ppermute(lower[-1] if lower else x, axis, pairs))
+        else:
+            upper.append(lax.ppermute(upper[-1] if upper else x, axis, back))
+    pieces = jnp.stack([*lower[::-1], x, *upper])
+    shift = lax.axis_index(axis) - len(lower)
+    pieces = pieces[(jnp.arange(devices) - shift) % devices]
+    return joined_along(pieces, dim)
 
 
 def layer_norm(values, gain, shift):
@@ -153,7 +175,7 @@
     full_weights = (
         lax.all_gather(partial_full[0], "fsdp", axis=0, tiled=True),
         lax.all_gather(partial_full[1], "fsdp", axis=0, tiled=True),
-        lax.all_gather(partial_full[2], "fsdp", axis=0, tiled=True),
+        collect(partial_full[2], "fsdp", 0),
         lax.all_gather(partial_full[3], "fsdp", axis=0, tiled=True),
     )
     mixing_full, output_full, expand_full, contract_full = full_weights

time: 1170 us -> 1060 us (0.906)
  waiting for transfers between devices: 725 us -> 588 us
  starting transfers between devices: 9.06 us -> 33.7 us
  blocking collectives: 154 us -> 133 us
  local copies, waits for them, and re-layouts: 71.4 us -> 91.4 us
    ppermute x0 -> x7, waiting for transfers between devices: none -> 175 us  [the longest x4 175 us: collect(): lower.append(lax.ppermute(lower[-1] if lower else x, axis, pairs))]
    reduce_scatter x1, waiting for transfers between devices: 151 us -> 31.4 us  [body(): lax.psum_scatter(grad_contract.astype(jnp.bfloat16), 'fsdp', scatter_dime...]
    all_gather x1, waiting for transfers between devices: 101 us -> 0.92 us  [body(): lax.all_gather(partial_full[0], 'fsdp', axis=0, tiled=True)]
    all_gather x1, waiting for transfers between devices: 115 us -> 50.4 us  [body(): lax.all_gather(partial_full[3], 'fsdp', axis=0, tiled=True)]
    all_gather x1 -> x0, waiting for transfers between devices: 48.9 us -> none  [body(): lax.all_gather(partial_full[2], 'fsdp', axis=0, tiled=True)]
    reduce_scatter x1, waiting for transfers between devices: 89.2 us -> 120 us  [body(): lax.psum_scatter(grad_mixing.astype(jnp.bfloat16), 'fsdp', scatter_dimens...]
    ppermute x0 -> x7, starting transfers between devices: none -> 21.2 us  [the longest x3 14.7 us: collect(): upper.append(lax.ppermute(upper[-1] if upper else x, axis, back))]
    reduce_scatter x1, waiting for transfers between devices: 0.01 us -> 20.6 us  [body(): lax.psum_scatter(summed_first[0].astype(jnp.bfloat16), 'seq', scatter_dim...]
  transfers between devices with their start and end apart: 16 -> 23, of which waited for: 12 -> 15; matrix products, arithmetic and copies ran while one was open for 19% -> 22% of each run, Pallas kernels for 0% -> 0%
where the time goes in v1:
time: 1060 us; the launch traced here: 1050 us
  waiting for transfers between devices  588 us (55%)
  matrix products  151 us (14%)
  blocking collectives  133 us (13%)
  local copies, waits for them, and re-layouts  91.4 us (9%)
  other arithmetic  40.4 us (4%)
  starting transfers between devices  33.7 us (3%)
  between operations  15.6 us (1%)
    ppermute x4, waiting for transfers between devices, collect(): lower.append(lax.ppermute(lower[-1] if lower else x, axis, pairs))  175 us
    reduce_scatter x1, waiting for transfers between devices, body(): lax.psum_scatter(grad_mixing.astype(jnp.bfloat16), 'fsdp', scatter_dimens...  120 us
    reduce_scatter x1, waiting for transfers between devices, body(): lax.psum_scatter(grad_expand.astype(jnp.bfloat16), 'fsdp', scatter_dimens...  106 us
    all_to_all x1, blocking collectives, body(): lax.all_to_all(packed_cot, 'seq', split_axis=1, concat_axis=2, tiled=True)  53.9 us
    all_gather x1, waiting for transfers between devices, body(): lax.all_gather(partial_full[3], 'fsdp', axis=0, tiled=True)  50.4 us
    psum x1, blocking collectives, body(): lax.psum((grad_first_gain, grad_first_shift, grad_mixing_bias, grad_outpu...  40.8 us
    unnamed x155, local copies, waits for them, and re-layouts  34.2 us
    reduce_scatter x1, waiting for transfers between devices, body(): lax.psum_scatter(grad_contract.astype(jnp.bfloat16), 'fsdp', scatter_dime...  31.4 us
  transfers between devices with their start and end apart: 23, of which 15 were waited for; matrix products, arithmetic and copies ran while one was open for 22% of the time, Pallas kernels for 0%

profile of v1, /device:TPU:0, one launch (start us, length us, event | category | flops | bytes accessed | tf_op | source)
XLA Modules:
  0.0 1053.4 jit_solution(10702376058551517211)
XLA Ops:
  8.7 11.7 %all_gather.21 = bf16[128,3072]{1,0:T(8,128)(2,1)} all-gather(bf16[128,768]{1,0:T(8,128)(2,1)} %param.30), channel_id=1, replica_groups=mesh['fsdp'=8,'seq'=4] {'seq'}, dimensions={1}, use_global_device_ids=true | all-gather | bytes 983040 | tf_op jit(solution)/shard_map/all_gather | solution.py:170
  20.5 8.6 all-gather.10.cloned.1.call-done
  30.5 6.5 all_gather.23
  37.1 20.2 %collective-permute-done = bf16[128,4096]{1,0:T(8,128)(2,1)S(1)} collective-permute-done((bf16[128,4096]{1,0:T(8,128)(2,1)}, bf16[128,4096]{1,0:T(8,128)(2,1)S(1)}, u32[]{:S(2)}, u32[]{:S(2)}) %collective-permute-start) | collective-permute-done | bytes 1048608 | tf_op jit(solution)/shard_map/ppermute | solution.py:25
  57.3 4.7 collective-permute-start.4
  62.0 48.5 %collective-permute-done.1 = bf16[128,4096]{1,0:T(8,128)(2,1)} collective-permute-done((bf16[128,4096]{1,0:T(8,128)(2,1)S(1)}, bf16[128,4096]{1,0:T(8,128)(2,1)}, u32[]{:S(2)}, u32[]{:S(2)}) %collective-permute-start.1) | collective-permute-done | bytes 1048608 | tf_op jit(solution)/shard_map/ppermute | solution.py:25
  115.3 64.4 %collective-permute-done.2 = bf16[128,4096]{1,0:T(8,128)(2,1)} collective-permute-done((bf16[128,4096]{1,0:T(8,128)(2,1)}, bf16[128,4096]{1,0:T(8,128)(2,1)}, u32[]{:S(2)}, u32[]{:S(2)}) %collective-permute-start.2) | collective-permute-done | bytes 1048608 | tf_op jit(solution)/shard_map/ppermute | solution.py:25
  185.9 7.8 collective-permute-start.6
  193.7 42.1 %collective-permute-done.3 = bf16[128,4096]{1,0:T(8,128)(2,1)} collective-permute-done((bf16[128,4096]{1,0:T(8,128)(2,1)}, bf16[128,4096]{1,0:T(8,128)(2,1)}, u32[]{:S(2)}, u32[]{:S(2)}) %collective-permute-start.3) | collective-permute-done | bytes 1048608 | tf_op jit(solution)/shard_map/ppermute | solution.py:25
  244.8 7.8 add_convert_fusion
  257.6 4.2 all-to-all-start
  268.6 30.0 %all-to-all-done = bf16[2,256,16,192]{1,3,0,2:T(8,128)(2,1)S(1)} async-done(((bf16[2,256,16,192]{1,3,0,2:T(8,128)(2,1)}), bf16[2,256,16,192]{1,3,0,2:T(8,128)(2,1)S(1)}, u32[]{:S(2)}, u32[]{:S(2)}) %all-to-all-start) | async-done | bytes 3145760 | tf_op jit(solution)/shard_map/all_to_all | solution.py:192
  298.7 4.1 copy.158
  302.7 4.9 all_to_all.51
  323.2 5.2 fusion.69
  335.3 4.2 all-to-all-start.1
  342.0 8.7 gather_fusion
  364.2 7.0 fusion.92
  371.2 50.4 %all-gather.14.cloned.1.call-done = bf16[4096,1024]{1,0:T(8,128)(2,1)} async-done(((bf16[512,1024]{1,0:T(8,128)(2,1)}), bf16[4096,1024]{1,0:T(8,128)(2,1)}) %all-gather.14.cloned.1.call-update) | async-done | bytes 8388624 | tf_op jit(solution)/shard_map/all_gather | solution.py:179
  421.6 13.9 %convert_reduce_fusion = (f32[4096]{0:T(1024)}, bf16[2,256,4096]{2,1,0:T(8,128)(2,1)S(1)}) fusion(f32[2,256,4096]{2,1,0:T(8,128)} %fusion.92, f32[4096]{0:T(1024)S(1)} %copy-done.58, bf16[2,256,1024]{2,1,0:T(8,128)(2,1)} %param.40, bf16[4096,1024]{1,0:T(8,128)(2,1)} %all-gather.14.cloned.1.call-done), kind=kOutput, calls=%fused_computation.26 | convolution fusion | flops 4343197696 | bytes 22052864 | tf_op jit(solution)/shard_map/ntd,id->nti/dot_general | solution.py:215
  435.5 9.8 multiply_reduce_fusion.2
  450.5 13.0 %bitcast_convert_fusion = bf16[4096,1024]{1,0:T(8,128)(2,1)} fusion(bf16[2,256,1024]{2,1,0:T(8,128)(2,1)S(1)} %copy-done.16, f32[2,256,4096]{2,1,0:T(8,128)} %fusion.92, f32[4096]{0:T(1024)S(1)} %copy-done.58), kind=kOutput, calls=%fused_computation.1 | convolution fusion | flops 4320133120 | bytes 17842176 | tf_op jit(solution)/shard_map/nti,ntd->id/dot_general | solution.py:213
  465.2 3.5 fusion.53
  471.3 3.5 all-to-all-start.2
  475.5 13.7 %all-to-all-done.2 = bf16[2,256,16,64]{1,3,0,2:T(8,128)(2,1)S(1)} async-done(((bf16[2,256,16,64]{1,3,0,2:T(8,128)(2,1)}), bf16[2,256,16,64]{1,3,0,2:T(8,128)(2,1)S(1)}, u32[]{:S(2)}, u32[]{:S(2)}) %all-to-all-start.2) | async-done | bytes 1048608 | tf_op jit(solution)/shard_map/all_to_all | solution.py:239
  491.3 8.5 fusion.98
  500.7 5.0 multiply_convert_fusion.1
  509.2 3.6 fusion.61
  515.2 10.9 %fusion.97 = (f32[2,4]{1,0:T(2,128)}, f32[2,4,512]{2,1,0:T(4,128)}, f32[2,4,512,1024]{3,2,1,0:T(8,128)}) fusion(f32[2,4,512,1024]{3,2,1,0:T(8,128)S(1)} %bitcast.134, f32[2,4,512]{2,1,0:T(4,128)} %bitcast.155, bf16[2,1024,4,192]{1,3,2,0:T(8,128)(2,1)} %copy-done.8, bf16[2,1024,4,64]{1,3,2,0:T(8,128)(2,1)} %copy-done.10), kind=kOutput, calls=%fused_computation.155 | convolution fusion | flops 553644032 | bytes 35160096 | tf_op jit(solution)/shard_map/nqhd,nkhd->nhqk/dot_general | solution.py:117
  526.1 8.0 multiply_convert_fusion
  534.2 3.6 fusion.44
  537.8 4.8 fusion.68
  542.6 4.4 fusion.43
  548.8 7.6 copy.170
  556.4 53.9 %all_to_all.66 = bf16[2,1024,4,192]{3,2,0,1:T(4,128)(2,1)} all-to-all(bf16[2,1024,4,192]{3,2,0,1:T(4,128)(2,1)} %copy.170), channel_id=1, replica_groups=mesh['fsdp'=8,'seq'=4] {'seq'}, dimensions={1} | all-to-all | bytes 6291456 | tf_op jit(solution)/shard_map/all_to_all | solution.py:241
  610.3 7.3 copy.172
  617.6 7.8 bitcast_convert_fusion.2
  627.0 9.3 bitcast_convert_fusion.1
  637.0 31.4 %reduce-scatter.21.cloned.1.call-done = bf16[512,1024]{1,0:T(8,128)(2,1)} async-done(((bf16[4096,1024]{1,0:T(8,128)(2,1)}), bf16[512,1024]{1,0:T(8,128)(2,1)}) %reduce-scatter.21.cloned.1.call-update) | async-done | bytes 1048592 | tf_op jit(solution)/shard_map/reduce_scatter | solution.py:264
  669.1 120.2 %reduce-scatter.9.cloned.1.call-done = bf16[128,3072]{1,0:T(8,128)(2,1)} async-done(((bf16[1024,3072]{1,0:T(8,128)(2,1)}), bf16[128,3072]{1,0:T(8,128)(2,1)}) %reduce-scatter.9.cloned.1.call-update) | async-done | bytes 786448 | tf_op jit(solution)/shard_map/reduce_scatter | solution.py:255
  789.4 12.2 %add_convert_fusion.1 = bf16[2,256,1024]{2,1,0:T(8,128)(2,1)} fusion(f32[2,256,1024]{2,1,0:T(8,128)S(1)} %copy-done.7, bf16[4096,1024]{1,0:T(8,128)(2,1)} %all-gather.14.cloned.1.call-done, f32[1024]{0:T(1024)S(1)} %copy-done.64, f32[2,256,4096]{2,1,0:T(8,128)} %fusion.92, f32[4096]{0:T(1024)S(1)} %copy-done.59), kind=kOutput, calls=%fused_computation.80 | convolution fusion | flops 4317511680 | bytes 19943424 | tf_op jit(solution)/shard_map/nti,id->ntd/dot_general | solution.py:208
  801.7 20.6 %pmax.7 = f32[4]{0:T(128)S(1)} all-reduce(f32[4]{0:T(128)S(1)} %maximum_reduce_fusion), channel_id=1, replica_groups=mesh['fsdp'=8,'seq'=4] {'fsdp'}, use_global_device_ids=true, to_apply=%region_41.42 | all-reduce | flops 4 | bytes 32 | tf_op jit(solution)/shard_map/pmax | solution.py:295
  824.7 7.9 copy.193
  836.3 105.5 %reduce-scatter.17.cloned.1.call-done = bf16[128,4096]{1,0:T(8,128)(2,1)} async-done(((bf16[1024,4096]{1,0:T(8,128)(2,1)}), bf16[128,4096]{1,0:T(8,128)(2,1)}) %reduce-scatter.17.cloned.1.call-update) | async-done | bytes 1048592 | tf_op jit(solution)/shard_map/reduce_scatter | solution.py:261
  941.9 7.0 fusion.99
  952.6 40.8 %all-reduce.2 = (f32[1024]{0:T(1024)}, f32[1024]{0:T(1024)}, f32[3072]{0:T(1024)}, f32[1024]{0:T(1024)}, f32[1024]{0:T(1024)}, /*index=5*/f32[1024]{0:T(1024)}, f32[4096]{0:T(1024)}, f32[1024]{0:T(1024)}) all-reduce(f32[1024]{0:T(1024)S(1)} %get-tuple-element.87, ...), channel_id=1, replica_groups=mesh['fsdp'=8,'seq'=4] {'fsdp','seq'}, use_global_device_ids=true, to_apply=%region_15.16 | all-reduce | flops 13312 | bytes 106496 | tf_op jit(solution)/shard_map/psum | solution.py:282
  996.6 20.6 %reduce-scatter.11.cloned.1.call-done = bf16[128,768]{1,0:T(8,128)(2,1)} async-done(((bf16[128,3072]{1,0:T(8,128)(2,1)}), bf16[128,768]{1,0:T(8,128)(2,1)}) %reduce-scatter.11.cloned.1.call-update) | async-done | bytes 196624 | tf_op jit(solution)/shard_map/reduce_scatter | solution.py:269
  1019.0 25.9 %reduce-scatter.19.cloned.1.call-done = bf16[128,1024]{1,0:T(8,128)(2,1)} async-done(((bf16[128,4096]{1,0:T(8,128)(2,1)}), bf16[128,1024]{1,0:T(8,128)(2,1)}) %reduce-scatter.19.cloned.1.call-update) | async-done | bytes 262160 | tf_op jit(solution)/shard_map/reduce_scatter | solution.py:275
  (256 shorter events, 112.9 us)
Async XLA Ops:
  7.2 176.5 %copy-start.2 = (bf16[2,256,1024]{2,1,0:T(8,128)(2,1)S(1)}, bf16[2,256,1024]{2,1,0:T(8,128)(2,1)}, u32[]{:S(2)}) copy-start(bf16[2,256,1024]{2,1,0:T(8,128)(2,1)} %param.27) | copy-start | bytes 3145732
  7.2 21.9 %all-gather.10.cloned.1.call-start = ((), (), s32[]{:S(2)}) async-start(), calls=%async_computation.14 | async-start | bytes 1310720 | tf_op jit(solution)/shard_map/all_gather | solution.py:172
  7.9 177.9 %all-gather.12.cloned.1.call-start = ((), (), s32[]{:S(2)}) async-start(), calls=%async_computation.15 | async-start | bytes 1310720 | tf_op jit(solution)/shard_map/all_gather | solution.py:173
  8.7 236.1 %all-gather.6.cloned.1.call-start = ((), (), s32[]{:S(2)}) async-start(), calls=%async_computation.12 | async-start | bytes 7077888 | tf_op jit(solution)/shard_map/all_gather | solution.py:176
  20.4 339.4 %all-gather.8.cloned.1.call-start = ((), (), s32[]{:S(2)}) async-start(), calls=%async_computation.13 | async-start | bytes 2359296 | tf_op jit(solution)/shard_map/all_gather | solution.py:177
  29.1 28.2 %collective-permute-start = (bf16[128,4096]{1,0:T(8,128)(2,1)}, bf16[128,4096]{1,0:T(8,128)(2,1)S(1)}, u32[]{:S(2)}, u32[]{:S(2)}) collective-permute-start(bf16[128,4096]{1,0:T(8,128)(2,1)} %all-gather.10.cloned.1.call-done), channel_id=1, source_target_pairs={{0,4},{4,8},{8,12},{12,16},{16,20},{20,24},{24,28},{28,0},{1,5},{5... | collective-permute-start | bytes 3145736 | tf_op jit(solution)/shard_map/ppermute | solution.py:25
  37.0 384.6 %all-gather.14.cloned.1.call-start = ((), (), s32[]{:S(2)}) async-start(), calls=%async_computation.16 | async-start | bytes 9437184 | tf_op jit(solution)/shard_map/all_gather | solution.py:179
  57.3 53.2 %collective-permute-start.1 = (bf16[128,4096]{1,0:T(8,128)(2,1)S(1)}, bf16[128,4096]{1,0:T(8,128)(2,1)}, u32[]{:S(2)}, u32[]{:S(2)}) collective-permute-start(bf16[128,4096]{1,0:T(8,128)(2,1)S(1)} %collective-permute-done), channel_id=1, source_target_pairs={{0,4},{4,8},{8,12},{12,16},{16,20},{20,24},{24,28},{28,0},{1,5},{5... | collective-permute-start | bytes 3145736 | tf_op jit(solution)/shard_map/ppermute | solution.py:25
  57.3 55.9 %collective-permute-start.4 = (bf16[128,4096]{1,0:T(8,128)(2,1)}, bf16[128,4096]{1,0:T(8,128)(2,1)S(1)}, u32[]{:S(2)}, u32[]{:S(2)}) collective-permute-start(bf16[128,4096]{1,0:T(8,128)(2,1)} %all-gather.10.cloned.1.call-done), channel_id=1, source_target_pairs={{4,0},{8,4},{12,8},{16,12},{20,16},{24,20},{28,24},{0,28},{5,1},{9... | collective-permute-start | bytes 3145736 | tf_op jit(solution)/shard_map/ppermute | solution.py:27
  110.4 69.3 %collective-permute-start.2 = (bf16[128,4096]{1,0:T(8,128)(2,1)}, bf16[128,4096]{1,0:T(8,128)(2,1)}, u32[]{:S(2)}, u32[]{:S(2)}) collective-permute-start(bf16[128,4096]{1,0:T(8,128)(2,1)} %collective-permute-done.1), channel_id=1, source_target_pairs={{0,4},{4,8},{8,12},{12,16},{16,20},{20,24},{24,28},{28,0},{1,5},{5... | collective-permute-start | bytes 3145736 | tf_op jit(solution)/shard_map/ppermute | solution.py:25
  113.1 129.6 %copy-start.24 = (bf16[128,4096]{1,0:T(8,128)(2,1)}, bf16[128,4096]{1,0:T(8,128)(2,1)S(1)}, u32[]{:S(2)}) copy-start(bf16[128,4096]{1,0:T(8,128)(2,1)S(1)} %collective-permute-done.4) | copy-start | bytes 3145732
  113.2 72.8 %collective-permute-start.5 = (bf16[128,4096]{1,0:T(8,128)(2,1)S(1)}, bf16[128,4096]{1,0:T(8,128)(2,1)}, u32[]{:S(2)}, u32[]{:S(2)}) collective-permute-start(bf16[128,4096]{1,0:T(8,128)(2,1)S(1)} %collective-permute-done.4), channel_id=1, source_target_pairs={{4,0},{8,4},{12,8},{16,12},{20,16},{24,20},{28,24},{0,28},{5,1},{9... | collective-permute-start | bytes 3145736 | tf_op jit(solution)/shard_map/ppermute | solution.py:27
  179.7 56.1 %collective-permute-start.3 = (bf16[128,4096]{1,0:T(8,128)(2,1)}, bf16[128,4096]{1,0:T(8,128)(2,1)}, u32[]{:S(2)}, u32[]{:S(2)}) collective-permute-start(bf16[128,4096]{1,0:T(8,128)(2,1)} %collective-permute-done.2), channel_id=1, source_target_pairs={{0,4},{4,8},{8,12},{12,16},{16,20},{20,24},{24,28},{28,0},{1,5},{5... | collective-permute-start | bytes 3145736 | tf_op jit(solution)/shard_map/ppermute | solution.py:25
  183.7 61.1 %copy-start.39 = (f32[2,256]{1,0:T(2,128)}, f32[2,256]{1,0:T(2,128)S(1)}, u32[]{:S(2)}) copy-start(f32[2,256]{1,0:T(2,128)S(1)} %broadcast_multiply_fusion.1) | copy-start | bytes 6148
  184.7 60.1 %copy-start.41 = (f32[2,256]{1,0:T(2,128)}, f32[2,256]{1,0:T(2,128)S(1)}, u32[]{:S(2)}) copy-start(f32[2,256]{1,0:T(2,128)S(1)} %fusion.93) | copy-start | bytes 6148
  185.9 58.9 %copy-start.46 = (f32[1024]{0:T(1024)S(1)}, f32[1024]{0:T(1024)}, u32[]{:S(2)}) copy-start(f32[1024]{0:T(1024)} %param.28) | copy-start | bytes 12292
  185.9 58.9 %copy-start.57 = (f32[3072]{0:T(1024)S(1)}, f32[3072]{0:T(1024)}, u32[]{:S(2)}) copy-start(f32[3072]{0:T(1024)} %param.31) | copy-start | bytes 36868
  185.9 58.9 %copy-start.60 = (f32[1024]{0:T(1024)S(1)}, f32[1024]{0:T(1024)}, u32[]{:S(2)}) copy-start(f32[1024]{0:T(1024)} %param.29) | copy-start | bytes 12292
  185.9 153.7 %collective-permute-start.6 = (bf16[128,4096]{1,0:T(8,128)(2,1)}, bf16[128,4096]{1,0:T(8,128)(2,1)}, u32[]{:S(2)}, u32[]{:S(2)}) collective-permute-start(bf16[128,4096]{1,0:T(8,128)(2,1)} %collective-permute-done.5), channel_id=1, source_target_pairs={{4,0},{8,4},{12,8},{16,12},{20,16},{24,20},{28,24},{0,28},{5,1},{9... | collective-permute-start | bytes 3145736 | tf_op jit(solution)/shard_map/ppermute | solution.py:27
  257.6 41.1 %all-to-all-start = ((bf16[2,256,16,192]{1,3,0,2:T(8,128)(2,1)}), bf16[2,256,16,192]{1,3,0,2:T(8,128)(2,1)S(1)}, u32[]{:S(2)}, u32[]{:S(2)}) async-start(bf16[2,256,16,192]{1,3,0,2:T(8,128)(2,1)} %copy.156), calls=%async_computation | async-start | bytes 6291456 | tf_op jit(solution)/shard_map/all_to_all | solution.py:192
  309.4 19.0 %copy-start.1 = (f32[2,4,512,512]{2,3,1,0:T(8,128)}, f32[2,4,512,512]{2,3,1,0:T(8,128)S(1)}, u32[]{:S(2)}) copy-start(f32[2,4,512,512]{2,3,1,0:T(8,128)S(1)} %get-tuple-element.109) | copy-start | bytes 25165828
  309.4 19.0 %copy-start.31 = (f32[2,4,512]{2,1,0:T(4,128)}, f32[2,4,512]{2,1,0:T(4,128)S(1)}, u32[]{:S(2)}) copy-start(f32[2,4,512]{2,1,0:T(4,128)S(1)} %get-tuple-element.108) | copy-start | bytes 49156
  314.1 14.3 %copy-start.33 = (f32[2,4,512]{2,1,0:T(4,128)}, f32[2,4,512]{2,1,0:T(4,128)S(1)}, u32[]{:S(2)}) copy-start(f32[2,4,512]{2,1,0:T(4,128)S(1)} %fusion.17) | copy-start | bytes 49156
  335.3 18.8 %all-to-all-start.1 = ((bf16[4,2,65536]{2,1,0:T(2,128)(2,1)}), bf16[4,2,65536]{2,1,0:T(2,128)(2,1)}, u32[]{:S(2)}, u32[]{:S(2)}) async-start(bf16[4,2,65536]{2,1,0:T(2,128)(2,1)} %reshape.370), calls=%async_computation.1 | async-start | bytes 2097152 | tf_op jit(solution)/shard_map/all_to_all | solution.py:99
  339.6 296.8 %reduce-scatter.13.cloned.1.call-start = ((), (), s32[]{:S(2)}) async-start(), calls=%async_computation.19 | async-start | bytes 2359296 | tf_op jit(solution)/shard_map/reduce_scatter | solution.py:258
  363.3 82.1 %copy-start.6 = (f32[2,256,1024]{2,1,0:T(8,128)}, f32[2,256,1024]{2,1,0:T(8,128)S(1)}, u32[]{:S(2)}) copy-start(f32[2,256,1024]{2,1,0:T(8,128)S(1)} %get-tuple-element.111) | copy-start | bytes 6291460
  363.7 81.7 %copy-start.49 = (f32[2,256]{1,0:T(2,128)}, f32[2,256]{1,0:T(2,128)S(1)}, u32[]{:S(2)}) copy-start(f32[2,256]{1,0:T(2,128)S(1)} %fusion.94) | copy-start | bytes 6148
  364.2 57.4 %copy-start.58 = (f32[4096]{0:T(1024)S(1)}, f32[4096]{0:T(1024)}, u32[]{:S(2)}) copy-start(f32[4096]{0:T(1024)} %param.37) | copy-start | bytes 49156
  435.5 9.8 copy-start.66
  450.5 217.9 %reduce-scatter.21.cloned.1.call-start = ((), (), s32[]{:S(2)}) async-start(), calls=%async_computation.23 | async-start | bytes 9437184 | tf_op jit(solution)/shard_map/reduce_scatter | solution.py:264
  471.3 18.0 %all-to-all-start.2 = ((bf16[2,256,16,64]{1,3,0,2:T(8,128)(2,1)}), bf16[2,256,16,64]{1,3,0,2:T(8,128)(2,1)S(1)}, u32[]{:S(2)}, u32[]{:S(2)}) async-start(bf16[2,256,16,64]{1,3,0,2:T(8,128)(2,1)} %copy.165), calls=%async_computation.2 | async-start | bytes 2097152 | tf_op jit(solution)/shard_map/all_to_all | solution.py:239
  474.8 314.5 %reduce-scatter.9.cloned.1.call-start = ((), (), s32[]{:S(2)}) async-start(), calls=%async_computation.17 | async-start | bytes 7077888 | tf_op jit(solution)/shard_map/reduce_scatter | solution.py:255
  474.9 24.9 %copy-start.28 = (f32[1,8,512]{2,1,0:T(8,128)}, f32[1,8,512]{2,1,0:T(8,128)S(1)}, u32[]{:S(2)}) copy-start(f32[1,8,512]{2,1,0:T(8,128)S(1)} %log_add_fusion.1) | copy-start | bytes 49156
  491.2 9.4 slice-start.5
  500.7 14.5 %slice-start = ((s8[16777216]{0:T(1024)(128)(4,1)}), s8[4194304]{0:T(1024)(128)(4,1)S(1)}, s32[]{:S(2)}) async-start(s8[16777216]{0:T(1024)(128)(4,1)} %bitcast.133), calls=%async_computation.25 | async-start | bytes 8388608
  500.7 14.5 %slice-start.1 = ((s8[16777216]{0:T(1024)(128)(4,1)}), s8[4194304]{0:T(1024)(128)(4,1)S(1)}, s32[]{:S(2)}) async-start(s8[16777216]{0:T(1024)(128)(4,1)} %bitcast.133), calls=%async_computation.26 | async-start | bytes 8388608
  500.7 14.5 %slice-start.2 = ((s8[16777216]{0:T(1024)(128)(4,1)}), s8[4194304]{0:T(1024)(128)(4,1)S(1)}, s32[]{:S(2)}) async-start(s8[16777216]{0:T(1024)(128)(4,1)} %bitcast.133), calls=%async_computation.27 | async-start | bytes 8388608
  625.5 316.3 %reduce-scatter.17.cloned.1.call-start = ((), (), s32[]{:S(2)}) async-start(), calls=%async_computation.21 | async-start | bytes 9437184 | tf_op jit(solution)/shard_map/reduce_scatter | solution.py:261
  636.3 32.8 %copy-start.51 = (f32[2,4]{1,0:T(2,128)S(1)}, f32[2,4]{1,0:T(2,128)}, u32[]{:S(2)}) copy-start(f32[2,4]{1,0:T(2,128)} %get-tuple-element.83) | copy-start | bytes 100
  636.3 32.8 %copy-start.52 = (f32[2,4]{1,0:T(2,128)S(1)}, f32[2,4]{1,0:T(2,128)}, u32[]{:S(2)}) copy-start(f32[2,4]{1,0:T(2,128)} %get-tuple-element.81) | copy-start | bytes 100
  636.3 153.1 %copy-start.59 = (f32[4096]{0:T(1024)S(1)}, f32[4096]{0:T(1024)}, u32[]{:S(2)}) copy-start(f32[4096]{0:T(1024)} %param.37) | copy-start | bytes 49156
  636.3 153.1 %copy-start.64 = (f32[1024]{0:T(1024)S(1)}, f32[1024]{0:T(1024)}, u32[]{:S(2)}) copy-start(f32[1024]{0:T(1024)} %param.39) | copy-start | bytes 12292
  636.3 357.0 %reduce-scatter.15.cloned.1.call-start = ((), (), s32[]{:S(2)}) async-start(), calls=%async_computation.20 | async-start | bytes 327680 | tf_op jit(solution)/shard_map/reduce_scatter | solution.py:272
  636.9 358.0 %reduce-scatter.23.cloned.1.call-start = ((), (), s32[]{:S(2)}) async-start(), calls=%async_computation.24 | async-start | bytes 1310720 | tf_op jit(solution)/shard_map/reduce_scatter | solution.py:278
  668.3 348.9 %reduce-scatter.11.cloned.1.call-start = ((), (), s32[]{:S(2)}) async-start(), calls=%async_computation.18 | async-start | bytes 983040 | tf_op jit(solution)/shard_map/reduce_scatter | solution.py:269
  789.3 34.6 %copy-start.25 = (bf16[128,768]{1,0:T(8,128)(2,1)S(1)}, bf16[128,768]{1,0:T(8,128)(2,1)}, u32[]{:S(2)}) copy-start(bf16[128,768]{1,0:T(8,128)(2,1)} %param.30) | copy-start | bytes 589828
  789.4 255.5 %reduce-scatter.19.cloned.1.call-start = ((), (), s32[]{:S(2)}) async-start(), calls=%async_computation.22 | async-start | bytes 1310720 | tf_op jit(solution)/shard_map/reduce_scatter | solution.py:275
  822.2 13.8 %copy-start.65 = (f32[4]{0:T(128)}, f32[4]{0:T(128)S(1)}, u32[]{:S(2)}) copy-start(f32[4]{0:T(128)S(1)} %pmax.7) | copy-start | bytes 52
  (48 other events, 226.7 us)
Sparse Core Ops, SparseCore 0:
  9.6 19.4 all-gather.9
  30.6 16.8 all-gather.11
  49.7 195.0 all-gather.5
  246.7 49.4 all-gather.7
  298.2 123.4 all-gather.13
  450.6 66.0 reduce-scatter.12
  520.3 147.9 reduce-scatter.20
  672.3 116.9 reduce-scatter.8
  793.4 148.3 reduce-scatter.16
  944.1 19.1 reduce-scatter.14
  965.9 25.2 reduce-scatter.22
  993.6 23.6 reduce-scatter.10
  1019.9 24.8 reduce-scatter.18
